TPU v7x, 256 devices: a whole 4x4x8 slice. The times are simulated.
256 devices in a mesh: blk: 4 (over y_hi, core), dp: 64 (over z, x, y_lo).
Axes of the slice: x: 4, y: 4 (y_hi: 2, y_lo: 2; y = y_hi * 2 + y_lo), z: 8, core: 2. Of those that a mesh axis runs over, the one named last changes fastest.
Arguments:
- fingerprints: bfloat16 [98304, 2048], P(('blk', 'dp')), may hold values from 0 to 3, as said below
- w_first: bfloat16 [2048, 1024], replicated, may hold values from -0.3125 to 0.3125
- w_second: bfloat16 [1024, 512], replicated, may hold values from -0.0625 to 0.0625
Outputs:
- grad_first: float32 [2048, 1024], P('dp')
- grad_second: float32 [1024, 512], P('dp')
Inputs may be any that keep to these rules, and one draw needn't show every extreme that they name: `fingerprints`: Non-negative feature weights; every molecule has a third or more of its features nonzero.
All inputs are finite; a program needn't handle non-finite values.
Results may differ from a plain program's by a relative error of at most 0.003.
Values may be sent and summed in bfloat16 or wider, within the bound.
A program may use at most 64 MiB of HBM per device.

v0:
```python
import math
import jax
import jax.numpy as jnp
from jax import lax
from jax.sharding import PartitionSpec as P


def pair_tile(mine_feats, mine_embed, mine_sqn, other, width):
    other_feats = other[:, :width]
    other_embed = other[:, width:]
    other_sqn = jnp.sum(jnp.square(other_feats.astype(jnp.float32)), axis=1)
    contract = (((1,), (1,)), ((), ()))
    inter = lax.dot_general(mine_feats, other_feats, contract, preferred_element_type=jnp.float32)
    tanimoto = inter / (mine_sqn[:, None] + other_sqn[None, :] - inter)
    scale = 1.0 / math.sqrt(mine_embed.shape[1])
    pred = (
        lax.dot_general(mine_embed, other_embed, contract, preferred_element_type=jnp.float32)
        * scale
    )
    return ((pred - tanimoto).astype(jnp.bfloat16), other_embed)


def column_product(left, right):
    return lax.dot_general(
        left, right, (((0,), (0,)), ((), ())), preferred_element_type=jnp.float32
    )


def per_device(fingerprints, w_first, w_second):
    tok_rows, width = fingerprints.shape
    blk_count = lax.axis_size("blk")
    dp_count = lax.axis_size("dp")
    group_rows = tok_rows * blk_count
    all_rows = group_rows * dp_count
    pre = jnp.dot(fingerprints, w_first, preferred_element_type=jnp.float32)
    sig = jax.nn.sigmoid(pre)
    hidden = (pre * sig).astype(jnp.bfloat16)
    embed = jnp.dot(hidden, w_second, preferred_element_type=jnp.float32).astype(jnp.bfloat16)
    mine_sqn = jnp.sum(jnp.square(fingerprints.astype(jnp.float32)), axis=1)
    packed = jnp.concatenate([fingerprints, embed], axis=1)
    resid, other_embed = pair_tile(
        fingerprints, embed, mine_sqn, lax.all_gather(packed, "blk", axis=0, tiled=True), width
    )
    summed = jnp.dot(resid, other_embed, preferred_element_type=jnp.float32)
    dembed = (summed * (2.0 / math.sqrt(group_rows * all_rows))).astype(jnp.bfloat16)
    dhidden = lax.dot_general(
        dembed, w_second, (((1,), (1,)), ((), ())), preferred_element_type=jnp.float32
    )
    dpre = (dhidden * sig * (1.0 + pre * (1.0 - sig))).astype(jnp.bfloat16)
    first_part = lax.psum_scatter(
        column_product(fingerprints, dpre), "dp", scatter_dimension=0, tiled=True
    )
    second_part = lax.psum_scatter(
        column_product(hidden, dembed), "dp", scatter_dimension=0, tiled=True
    )
    grad_first, grad_second = lax.psum((first_part, second_part), "blk")
    return (grad_first, grad_second)


def solution(mesh):
    in_specs = (P(("blk", "dp"), None), P(), P())
    out_specs = (P("dp", None), P("dp", None))
    return jax.shard_map(
        per_device, mesh=mesh, in_specs=in_specs, out_specs=out_specs, check_vma=False
    )
```

profile of v0, /device:TPU:1, one launch (start us, length us, event | category | flops | bytes accessed | tf_op | source)
XLA Modules:
  0.0 816.7 jit_solution(17026861810282639801)
XLA Ops:
  7.2 0.0 copy-start
  7.2 0.0 all-gather.2.cloned.1.call-start
  7.2 4.5 fusion.22
  11.8 0.0 copy-start.2
  11.8 1.1 copy-done.2
  12.9 0.0 copy-done
  12.9 0.0 copy-start.1
  12.9 0.6 convolution_convert_fusion
  13.5 0.8 copy-done.1
  14.3 1.5 pad_maximum_fusion
  15.8 0.0 all-gather.2.cloned.1.call-update
  15.9 0.0 reduce-scatter.7.cloned.1.call-start
  15.9 0.4 multiply_reduce_fusion.1
  16.3 65.9 %all-gather.2.cloned.1.call-done = bf16[1536,2560]{1,0:T(8,128)(2,1)} async-done(((bf16[384,2560]{1,0:T(8,128)(2,1)}), bf16[1536,2560]{1,0:T(8,128)(2,1)}) %all-gather.2.cloned.1.call-update) | async-done | bytes 7864336 | tf_op jit(solution)/shard_map/all_gather | solution.py:42
  82.2 4.1 multiply_reduce_fusion
  86.2 7.7 fusion.3
  93.9 4.4 fusion.13
  98.4 6.5 convolution_bitcast_fusion
  104.9 9.3 %copy.7 = f32[2048,1024]{1,0:T(8,128)} copy(f32[2048,1024]{0,1:T(8,128)} %convolution_bitcast_fusion) | data formatting | bytes 16777216
  114.2 0.0 copy-start.3
  114.2 0.0 reduce-scatter.7.cloned.1.call-update
  114.2 0.0 reduce-scatter.5.cloned.1.call-start
  114.3 1.3 copy-done.3
  115.6 2.2 fusion.21
  117.8 0.0 reduce-scatter.5.cloned.1.call-update
  117.8 0.0 all-reduce.2.cloned.1.call-start
  117.9 283.1 %reduce-scatter.7.cloned.1.call-done = f32[32,1024]{1,0:T(8,128)} async-done(((f32[2048,1024]{1,0:T(8,128)}), f32[32,1024]{1,0:T(8,128)}) %reduce-scatter.7.cloned.1.call-update) | async-done | bytes 131088
  401.0 1.9 copy.8
  402.8 0.0 all-reduce.2.cloned.1.call-update
  402.9 309.9 %reduce-scatter.5.cloned.1.call-done = f32[16,512]{1,0:T(8,128)} async-done(((f32[1024,512]{1,0:T(8,128)}), f32[16,512]{1,0:T(8,128)}) %reduce-scatter.5.cloned.1.call-update) | async-done | bytes 32784 | tf_op jit(solution)/shard_map/reduce_scatter | solution.py:53
  712.7 63.9 %psum.15 = f32[16,512]{1,0:T(8,128)} all-reduce(f32[16,512]{1,0:T(8,128)} %reduce-scatter.5.cloned.1.call-done), channel_id=1, replica_groups=mesh['blk'=4,'dp'=64] {'blk'}, use_global_device_ids=true, to_apply=%region_5.0 | all-reduce | flops 8192 | bytes 65536 | tf_op jit(solution)/shard_map/psum | solution.py:56
  776.6 31.6 %all-reduce.2.cloned.1.call-done = f32[32,1024]{0,1:T(8,128)} async-done(((f32[32,1024]{0,1:T(8,128)}), f32[32,1024]{0,1:T(8,128)}) %all-reduce.2.cloned.1.call-update) | async-done | bytes 131088 | tf_op jit(solution)/shard_map/psum | solution.py:56
  808.3 1.9 copy.6
Async XLA Ops:
  7.2 5.8 copy-start
  7.2 75.0 %all-gather.2.cloned.1.call-start = ((), (), s32[]{:S(2)}) async-start(), calls=%async_computation.2 | async-start | bytes 9830400 | tf_op jit(solution)/shard_map/all_gather | solution.py:42
  11.8 1.2 copy-start.2
  12.9 1.4 copy-start.1
  15.9 385.1 %reduce-scatter.7.cloned.1.call-start = ((), (), s32[]{:S(2)}) async-start(), calls=%async_computation.5 | async-start | bytes 8519680
  114.2 1.4 copy-start.3
  114.2 598.5 %reduce-scatter.5.cloned.1.call-start = ((), (), s32[]{:S(2)}) async-start(), calls=%async_computation.4 | async-start | bytes 2129920 | tf_op jit(solution)/shard_map/reduce_scatter | solution.py:53
  117.8 690.5 %all-reduce.2.cloned.1.call-start = ((), (), s32[]{:S(2)}) async-start(), calls=%async_computation.3 | async-start | bytes 1048576 | tf_op jit(solution)/shard_map/psum | solution.py:56
Sparse Core Ops, SparseCore 0:
  16.0 66.1 all-gather.1
  114.3 286.5 reduce-scatter.6
  403.5 309.2 reduce-scatter.4
  715.4 92.7 all-reduce.1
where the time goes:
time: 817 us
  waiting for transfers between devices  691 us (85%)
  blocking collectives  63.9 us (8%)
  matrix products  26 us (3%)
  local copies, waits for them, and re-layouts  16.3 us (2%)
  between operations  13.8 us (2%)
    reduce_scatter x1, waiting for transfers between devices, per_device(): lax.psum_scatter(column_product(hidden, dembed), 'dp', scatter_dimension=...  310 us
    unnamed x5, waiting for transfers between devices  283 us
    all_gather x1, waiting for transfers between devices, per_device(): lax.all_gather(packed, 'blk', axis=0, tiled=True)  65.9 us
    psum x1, blocking collectives, per_device(): grad_first, grad_second = lax.psum((first_part, second_part), 'blk')  63.9 us
    psum x1, waiting for transfers between devices, per_device(): grad_first, grad_second = lax.psum((first_part, second_part), 'blk')  31.6 us
    unnamed x11, local copies, waits for them, and re-layouts  16.3 us
  transfers between devices with their start and end apart: 4, of which 4 were waited for; matrix products, arithmetic and copies ran while one was open for 1% of the time, Pallas kernels for 0%

commit v1 on v0

--- a/solution.py
+++ b/solution.py
@@ -39,7 +39,13 @@
     mine_sqn = jnp.sum(jnp.square(fingerprints.astype(jnp.float32)), axis=1)
     packed = jnp.concatenate([fingerprints, embed], axis=1)
     resid, other_embed = pair_tile(
-        fingerprints, embed, mine_sqn, lax.all_gather(packed, "blk", axis=0, tiled=True), width
+        fingerprints,
+        embed,
+        mine_sqn,
+        jnp.concatenate(
+            lax.all_to_all(jnp.stack([packed] * lax.axis_size("blk")), "blk", 0, 0), axis=0
+        ),
+        width,
     )
     summed = jnp.dot(resid, other_embed, preferred_element_type=jnp.float32)
     dembed = (summed * (2.0 / math.sqrt(group_rows * all_rows))).astype(jnp.bfloat16)

time: 817 us -> 851 us (1.042)
  waiting for transfers between devices: 691 us -> 713 us
  starting transfers between devices: 0.16 us -> 8.81 us
    all_to_all x0 -> x1, waiting for transfers between devices: none -> 87.8 us  [per_device(): lax.all_to_all(jnp.stack([packed] * lax.axis_size('blk')), 'blk', 0, 0)]
    all_gather x1 -> x0, waiting for transfers between devices: 65.9 us -> none  [per_device(): lax.all_gather(packed, 'blk', axis=0, tiled=True)]
    all_to_all x0 -> x1, starting transfers between devices: none -> 8.72 us  [per_device(): lax.all_to_all(jnp.stack([packed] * lax.axis_size('blk')), 'blk', 0, 0)]
    unnamed x5 -> x4, waiting for transfers between devices: 283 us -> 283 us
where the time goes in v1:
time: 851 us
  waiting for transfers between devices  713 us (84%)
  blocking collectives  65.2 us (8%)
  matrix products  24.9 us (3%)
  local copies, waits for them, and re-layouts  20.1 us (2%)
  between operations  13.8 us (2%)
  starting transfers between devices  8.81 us (1%)
    reduce_scatter x1, waiting for transfers between devices, per_device(): lax.psum_scatter(column_product(hidden, dembed), 'dp', scatter_dimension=...  310 us
    unnamed x4, waiting for transfers between devices  283 us
    all_to_all x1, waiting for transfers between devices, per_device(): lax.all_to_all(jnp.stack([packed] * lax.axis_size('blk')), 'blk', 0, 0)  87.8 us
    psum x1, blocking collectives, per_device(): grad_first, grad_second = lax.psum((first_part, second_part), 'blk')  65.2 us
    psum x1, waiting for transfers between devices, per_device(): grad_first, grad_second = lax.psum((first_part, second_part), 'blk')  32.7 us
  transfers between devices with their start and end apart: 4, of which 4 were waited for; matrix products, arithmetic and copies ran while one was open for 1% of the time, Pallas kernels for 0%

profile of v1, /device:TPU:1, one launch (start us, length us, event | category | flops | bytes accessed | tf_op | source)
XLA Modules:
  0.0 850.5 jit_solution(11085398927850381224)
XLA Ops:
  7.2 0.0 copy-start
  7.2 4.5 fusion.22
  11.7 0.0 copy-start.2
  11.7 1.1 copy-done.2
  12.9 0.0 copy-done
  12.9 0.0 copy-start.1
  12.9 0.6 convolution_convert_fusion
  13.5 0.8 copy-done.1
  14.3 0.1 pad_maximum_fusion
  14.4 3.8 stack.2
  18.2 8.7 %all-to-all-start = ((bf16[4,384,2560]{2,1,0:T(8,128)(2,1)}), bf16[4,384,2560]{2,1,0:T(8,128)(2,1)}, u32[]{:S(2)}, u32[]{:S(2)}) async-start(bf16[4,384,2560]{2,1,0:T(8,128)(2,1)} %stack.2), calls=%async_computation | async-start | bytes 15728640 | tf_op jit(solution)/shard_map/all_to_all | solution.py:46
  26.9 0.0 reduce-scatter.7.cloned.1.call-start
  26.9 0.4 multiply_reduce_fusion.1
  27.3 87.8 %all-to-all-done = bf16[4,384,2560]{2,1,0:T(8,128)(2,1)} async-done(((bf16[4,384,2560]{2,1,0:T(8,128)(2,1)}), bf16[4,384,2560]{2,1,0:T(8,128)(2,1)}, u32[]{:S(2)}, u32[]{:S(2)}) %all-to-all-start) | async-done | bytes 7864352 | tf_op jit(solution)/shard_map/all_to_all | solution.py:46
  115.2 4.1 multiply_reduce_fusion
  119.2 6.9 fusion.3
  126.1 4.1 fusion.13
  130.3 6.5 convolution_bitcast_fusion
  136.8 9.3 %copy.10 = f32[2048,1024]{1,0:T(8,128)} copy(f32[2048,1024]{0,1:T(8,128)} %convolution_bitcast_fusion) | data formatting | bytes 16777216
  146.1 0.0 copy-start.3
  146.1 0.0 reduce-scatter.7.cloned.1.call-update
  146.1 0.0 reduce-scatter.5.cloned.1.call-start
  146.2 1.3 copy-done.3
  147.5 2.2 fusion.21
  149.7 0.0 reduce-scatter.5.cloned.1.call-update
  149.7 0.0 all-reduce.2.cloned.1.call-start
  149.8 282.7 %reduce-scatter.7.cloned.1.call-done = f32[32,1024]{1,0:T(8,128)} async-done(((f32[2048,1024]{1,0:T(8,128)}), f32[32,1024]{1,0:T(8,128)}) %reduce-scatter.7.cloned.1.call-update) | async-done | bytes 131088
  432.5 1.9 copy.11
  434.4 0.0 all-reduce.2.cloned.1.call-update
  434.4 309.8 %reduce-scatter.5.cloned.1.call-done = f32[16,512]{1,0:T(8,128)} async-done(((f32[1024,512]{1,0:T(8,128)}), f32[16,512]{1,0:T(8,128)}) %reduce-scatter.5.cloned.1.call-update) | async-done | bytes 32784 | tf_op jit(solution)/shard_map/reduce_scatter | solution.py:59
  744.2 65.2 %psum.15 = f32[16,512]{1,0:T(8,128)} all-reduce(f32[16,512]{1,0:T(8,128)} %reduce-scatter.5.cloned.1.call-done), channel_id=1, replica_groups=mesh['blk'=4,'dp'=64] {'blk'}, use_global_device_ids=true, to_apply=%region_5.0 | all-reduce | flops 8192 | bytes 65536 | tf_op jit(solution)/shard_map/psum | solution.py:62
  809.4 32.7 %all-reduce.2.cloned.1.call-done = f32[32,1024]{0,1:T(8,128)} async-done(((f32[32,1024]{0,1:T(8,128)}), f32[32,1024]{0,1:T(8,128)}) %all-reduce.2.cloned.1.call-update) | async-done | bytes 131088 | tf_op jit(solution)/shard_map/psum | solution.py:62
  842.1 1.9 copy.8
Async XLA Ops:
  7.2 5.7 copy-start
  11.7 1.2 copy-start.2
  12.9 1.4 copy-start.1
  18.2 97.0 %all-to-all-start = ((bf16[4,384,2560]{2,1,0:T(8,128)(2,1)}), bf16[4,384,2560]{2,1,0:T(8,128)(2,1)}, u32[]{:S(2)}, u32[]{:S(2)}) async-start(bf16[4,384,2560]{2,1,0:T(8,128)(2,1)} %stack.2), calls=%async_computation | async-start | bytes 15728640 | tf_op jit(solution)/shard_map/all_to_all | solution.py:46
  26.9 405.6 %reduce-scatter.7.cloned.1.call-start = ((), (), s32[]{:S(2)}) async-start(), calls=%async_computation.5 | async-start | bytes 8519680
  146.1 1.4 copy-start.3
  146.1 598.1 %reduce-scatter.5.cloned.1.call-start = ((), (), s32[]{:S(2)}) async-start(), calls=%async_computation.4 | async-start | bytes 2129920 | tf_op jit(solution)/shard_map/reduce_scatter | solution.py:59
  149.7 692.4 %all-reduce.2.cloned.1.call-start = ((), (), s32[]{:S(2)}) async-start(), calls=%async_computation.3 | async-start | bytes 1048576 | tf_op jit(solution)/shard_map/psum | solution.py:62
Sparse Core Ops, SparseCore 0:
  146.2 286.2 reduce-scatter.6
  435.0 309.1 reduce-scatter.4
  747.1 94.9 all-reduce.1
